TPU v7x, 32 devices: a whole 2x2x4 slice. The times are simulated.
32 devices in a mesh: node: 4 (over y, x), leaf: 8 (over z, core).
Axes of the slice: x: 2, y: 2, z: 4, core: 2. Of those that a mesh axis runs over, the one named last changes fastest.
Arguments:
- density: bfloat16 [128, 8, 128, 256], P('leaf', 'node'), parts along dimension 1, may hold values from -6 to 6
- near_tiles: bfloat16 [128, 6, 8, 128, 128], P('leaf', None, 'node'), parts along dimension 2, may hold values from -0.15625 to 0.15625
- neighbours: int32 [128, 6], P('leaf'), may hold values from 0 to 127, as said below
- counts: int32 [128], P('leaf'), may hold values from 3 to 6, as said below
- leaf_basis: bfloat16 [128, 8, 32, 128], P('leaf', 'node'), parts along dimension 1, may hold values from -0.375 to 0.375
- leaf_transfer: float32 [128, 8, 32, 32], P('leaf', 'node'), parts along dimension 1, may hold values from -0.1875 to 0.1875
- admissible: int32 [8, 7], P('leaf'), may hold values from 0 to 7, as said below
- top_out: float32 [8, 8, 32, 32], P('leaf', 'node'), parts along dimension 1, may hold values from -0.75 to 0.75
- top_in: float32 [8, 8, 32, 32], P('leaf', 'node'), parts along dimension 1, may hold values from -0.25 to 0.25
- coupling: float32 [8, 7, 8, 32, 32], P('leaf', None, 'node'), parts along dimension 2, may hold values from -0.25 to 0.25
- down_transfer: float32 [128, 8, 32, 32], P('leaf', 'node'), parts along dimension 1, may hold values from -0.75 to 0.75
- out_basis: bfloat16 [128, 8, 32, 128], P('leaf', 'node'), parts along dimension 1, may hold values from -0.75 to 0.75
Outputs:
- potential: bfloat16 [128, 8, 128, 256], P('leaf', 'node'), parts along dimension 1
There are 4 independent parts, one for each index of `node`. A program takes and returns all parts, laid end to end along the dimension named above; an argument that names none is the same for every part. Nothing has to cross between parts.
Inputs may be any that keep to these rules, and one draw needn't show every extreme that they name: `neighbours`: slot 0 is the leaf itself; every neighbour lies within 4 leaf indices of its leaf; slots 1 and 2 are the leaves 4 below and above, clipped to the surface's range. `counts`: the number of live leading slots of each leaf. `admissible`: the 7 entries of row d are distinct and differ from d; slot 0 is d - 1 and slot 1 is d + 1, both modulo 8.
All inputs are finite; a program needn't handle non-finite values.
Results may differ from a plain program's by a relative error of at most 0.0045.
Values may be sent and summed in bfloat16 or wider, within the bound.
A program may use at most 128 MiB of HBM per device.

v0:
```python
import jax
import jax.numpy as jnp
from jax import lax
from jax.sharding import PartitionSpec as P

NEAR = 6


def from_behind(block, axis, distance):
    devices = range(lax.axis_size(axis))
    route = [(i - distance, i) for i in devices if i - distance in devices]
    return lax.ppermute(block, axis, route)


def complex_product(pattern, first, second, precision):

    def single(left_side, right_side):
        return jnp.einsum(
            pattern, left_side, right_side, precision=precision, preferred_element_type=jnp.float32
        )

    return (
        single(first[0], second[0]) - single(first[1], second[1]),
        single(first[0], second[1]) + single(first[1], second[0]),
    )


def shards(
    density,
    near_tiles,
    neighbours,
    counts,
    leaf_basis,
    leaf_transfer,
    admissible,
    top_out,
    top_in,
    coupling,
    down_transfer,
    out_basis,
):
    highest = lax.Precision.HIGHEST
    leaf_count = density.shape[0]
    coef = complex_product(
        "lkb,lbr->lkr", (leaf_basis[:, 0], leaf_basis[:, 1]), (density[:, 0], density[:, 1]), None
    )
    root = complex_product("lij,ljr->ir", (leaf_transfer[:, 0], leaf_transfer[:, 1]), coef, highest)
    root_stack = jnp.stack([root[0], root[1]])[None]
    top_term = complex_product("ij,jr->ir", (top_out[0, 0], top_out[0, 1]), root, highest)
    top_stack = jnp.stack([top_term[0], top_term[1]])
    root_coefs = lax.all_gather(root_stack, "leaf", axis=0, tiled=True)
    global_sum = lax.psum(top_stack, "leaf")
    picked = jnp.take(root_coefs, admissible[0], axis=0)
    far_field = complex_product(
        "fij,fjr->ir", (coupling[0, :, 0], coupling[0, :, 1]), (picked[:, 0], picked[:, 1]), highest
    )
    top_part = complex_product(
        "ij,jr->ir", (top_in[0, 0], top_in[0, 1]), (global_sum[0], global_sum[1]), highest
    )
    far_field = (far_field[0] + top_part[0], far_field[1] + top_part[1])
    down_pair = complex_product(
        "lij,jr->lir", (down_transfer[:, 0], down_transfer[:, 1]), far_field, highest
    )
    down_coefs = jnp.stack([down_pair[0], down_pair[1]], axis=1).astype(jnp.bfloat16)
    far_part = complex_product(
        "lkb,lkr->lbr",
        (out_basis[:, 0], out_basis[:, 1]),
        (down_coefs[:, 0], down_coefs[:, 1]),
        None,
    )
    below = from_behind(density, "leaf", 1)
    above = from_behind(density, "leaf", -1)
    extended = jnp.concatenate([below, density, above], axis=0)
    local_index = neighbours - lax.axis_index("leaf") * leaf_count + leaf_count
    totals = (far_part[0], far_part[1])
    for column in range(NEAR):

        def add_column(current, column=column):
            pieces = jnp.take(extended, local_index[:, column], axis=0)
            term = complex_product(
                "lab,lbr->lar",
                (near_tiles[:, column, 0], near_tiles[:, column, 1]),
                (pieces[:, 0], pieces[:, 1]),
                None,
            )
            live_mask = (counts > column).astype(jnp.float32)[:, None, None]
            return (current[0] + live_mask * term[0], current[1] + live_mask * term[1])

        totals = lax.cond(jnp.any(counts > column), add_column, lambda current: current, totals)
    return jnp.stack([totals[0], totals[1]], axis=1).astype(jnp.bfloat16)


def solution(mesh):
    in_specs = (
        P("leaf", "node", None, None),
        P("leaf", None, "node", None, None),
        P("leaf", None),
        P("leaf"),
        P("leaf", "node", None, None),
        P("leaf", "node", None, None),
        P("leaf", None),
        P("leaf", "node", None, None),
        P("leaf", "node", None, None),
        P("leaf", None, "node", None, None),
        P("leaf", "node", None, None),
        P("leaf", "node", None, None),
    )
    out_specs = P("leaf", "node", None, None)
    return jax.shard_map(shards, mesh=mesh, in_specs=in_specs, out_specs=out_specs, check_vma=False)
```

profile of v0, /device:TPU:24, one launch (start us, length us, event | category | flops | bytes accessed | tf_op | source)
XLA Modules:
  0.0 212.7 jit_solution(17887737348616619812)
XLA Ops:
  6.5 2.0 collective-permute-start
  8.6 3.6 %collective-permute-start.1 = (bf16[16,2,128,256]{3,2,1,0:T(8,128)(2,1)}, bf16[16,2,128,256]{3,2,1,0:T(8,128)(2,1)}, u32[]{:S(2)}, u32[]{:S(2)}) collective-permute-start(bf16[16,2,128,256]{3,2,1,0:T(8,128)(2,1)} %param.26), channel_id=1, source_target_pairs={{1,0},{2,1},{3,2},{4,3},{5,4},{6,5},{7,6},{9,8},{10,9},{11,10},{12... | collective-permute-start | bytes 6291464 | tf_op jit(solution)/shard_map/ppermute | solution.py:12
  20.0 27.4 %all-gather = f32[16,32,256]{2,1,0:T(8,128)S(1)} all-gather(f32[2,32,256]{2,1,0:T(8,128)S(1)} %pad_maximum_fusion.1), channel_id=2, replica_groups=mesh['node'=4,'leaf'=8] {'leaf'}, dimensions={0}, use_global_device_ids=true | all-gather | bytes 589824 | tf_op jit(solution)/shard_map/all_gather | solution.py:51
  54.0 19.9 %all-reduce.2.cloned.1.call-done = f32[2,32,256]{2,1,0:T(8,128)} async-done(((f32[2,32,256]{2,1,0:T(8,128)}), f32[2,32,256]{2,1,0:T(8,128)}) %all-reduce.2.cloned.1.call-update) | async-done | bytes 65552 | tf_op jit(solution)/shard_map/psum | solution.py:52
  83.2 3.3 %constant_dynamic-update-slice_fusion.2 = bf16[48,2,128,256]{3,2,1,0:T(8,128)(2,1)} fusion(bf16[16,2,128,256]{3,2,1,0:T(8,128)(2,1)} %collective-permute-done), kind=kLoop, calls=%fused_computation.207 | loop fusion | bytes 4194304
  88.0 3.2 %constant_dynamic-update-slice_fusion = bf16[48,2,128,256]{3,2,1,0:T(8,128)(2,1)} fusion(bf16[48,2,128,256]{3,2,1,0:T(8,128)(2,1)} %constant_dynamic-update-slice_fusion.1, bf16[16,2,128,256]{3,2,1,0:T(8,128)(2,1)} %collective-permute-done.1), kind=kLoop, calls=%fused_computation.205 | loop fusion | bytes 4194304 | tf_op jit(solution)/shard_map/concatenate | solution.py:73
  91.2 18.1 %conditional.6 = ((f32[16,128,256]{1,2,0:T(8,128)S(1)}, f32[16,128,256]{1,2,0:T(8,128)})) conditional(s32[]{:T(128)} %convert_element_type.43, (f32[16,128,256]{1,2,0:T(8,128)S(1)}, f32[16,128,256]{1,2,0:T(8,128)}) %tuple.57, (s32[16]{0:T(128)S(1)}, s32[16,6]{0,1:T(8,128)S(1)}, bf16[48,2,128,256]{3,2,1,0:T(8,128)(2,1)}, ...), branch_computations={%region_7.8_spmd, %region_8.10_spmd} | conditional | flops 541066368 | bytes 52434416 | solution.py:89
  91.2 4.9 %gather_fusion = bf16[16,2,128,256]{3,2,1,0:T(8,128)(2,1)} fusion(bf16[48,2,128,256]{3,2,1,0:T(8,128)(2,1)} %get-tuple-element.116, s32[1024]{0:T(1024)S(1)} %pad_clamp_fusion), kind=kCustom, calls=%fused_computation.clone | custom fusion | bytes 4194368 | tf_op jit(solution)/shard_map/cond/branch_1_fun/jit(_take)/gather | solution.py:79
  96.1 4.0 %copy.60 = bf16[16,2,128,256]{2,3,0,1:T(8,128)(2,1)} copy(bf16[16,2,128,256]{3,2,1,0:T(8,128)(2,1)} %gather_fusion) | data formatting | bytes 4194304 | tf_op jit(solution)/shard_map/cond/branch_1_fun/jit(_take)/gather | solution.py:79
  100.0 1.9 broadcast_select_fusion
  103.6 1.8 bitcast_add_fusion
  105.5 1.9 fusion
  107.4 1.9 bitcast_add_fusion.1
  109.3 18.1 %conditional.7 = ((f32[16,128,256]{1,2,0:T(8,128)S(1)}, f32[16,128,256]{1,2,0:T(8,128)})) conditional(s32[]{:T(128)} %convert_element_type.42, (f32[16,128,256]{1,2,0:T(8,128)S(1)}, f32[16,128,256]{1,2,0:T(8,128)}) %get-tuple-element.338, (s32[16]{0:T(128)S(1)}, s32[16,6]{0,1:T(8,128)S(1)}, bf16[48,2,128,256]{3,2,1,0:T(8,128)(2,1)}, ...), branch_computations={%region_9.11_spmd, %region_10.12_spmd} | conditional | flops 541066368 | bytes 52434416 | solution.py:89
  109.3 4.9 %gather_fusion.1 = bf16[16,2,128,256]{3,2,1,0:T(8,128)(2,1)} fusion(bf16[48,2,128,256]{3,2,1,0:T(8,128)(2,1)} %get-tuple-element.122, s32[1024]{0:T(1024)S(1)} %pad_clamp_fusion.1), kind=kCustom, calls=%fused_computation.1.clone | custom fusion | bytes 4194368 | tf_op jit(solution)/shard_map/cond/branch_1_fun/jit(_take)/gather | solution.py:79
  114.2 4.0 %copy.61 = bf16[16,2,128,256]{2,3,0,1:T(8,128)(2,1)} copy(bf16[16,2,128,256]{3,2,1,0:T(8,128)(2,1)} %gather_fusion.1) | data formatting | bytes 4194304 | tf_op jit(solution)/shard_map/cond/branch_1_fun/jit(_take)/gather | solution.py:79
  118.1 1.9 broadcast_select_fusion.1
  121.7 1.9 bitcast_add_fusion.2
  123.6 1.9 fusion.2
  125.5 1.9 bitcast_add_fusion.3
  127.4 18.1 %conditional.8 = ((f32[16,128,256]{1,2,0:T(8,128)S(1)}, f32[16,128,256]{1,2,0:T(8,128)})) conditional(s32[]{:T(128)} %convert_element_type.41, (f32[16,128,256]{1,2,0:T(8,128)S(1)}, f32[16,128,256]{1,2,0:T(8,128)}) %get-tuple-element.339, (s32[16]{0:T(128)S(1)}, s32[16,6]{0,1:T(8,128)S(1)}, bf16[48,2,128,256]{3,2,1,0:T(8,128)(2,1)}, ...), branch_computations={%region_11.13_spmd, %region_12.14_spmd} | conditional | flops 541066368 | bytes 52434416 | solution.py:89
  127.4 4.9 %gather_fusion.2 = bf16[16,2,128,256]{3,2,1,0:T(8,128)(2,1)} fusion(bf16[48,2,128,256]{3,2,1,0:T(8,128)(2,1)} %get-tuple-element.128, s32[1024]{0:T(1024)S(1)} %pad_clamp_fusion.2), kind=kCustom, calls=%fused_computation.2.clone | custom fusion | bytes 4194368 | tf_op jit(solution)/shard_map/cond/branch_1_fun/jit(_take)/gather | solution.py:79
  132.3 4.0 %copy.62 = bf16[16,2,128,256]{2,3,0,1:T(8,128)(2,1)} copy(bf16[16,2,128,256]{3,2,1,0:T(8,128)(2,1)} %gather_fusion.2) | data formatting | bytes 4194304 | tf_op jit(solution)/shard_map/cond/branch_1_fun/jit(_take)/gather | solution.py:79
  136.3 1.9 broadcast_select_fusion.2
  139.9 1.8 bitcast_add_fusion.4
  141.7 1.9 fusion.4
  143.6 1.9 bitcast_add_fusion.5
  145.5 18.1 %conditional.9 = ((f32[16,128,256]{1,2,0:T(8,128)S(1)}, f32[16,128,256]{1,2,0:T(8,128)})) conditional(s32[]{:T(128)} %convert_element_type.40, (f32[16,128,256]{1,2,0:T(8,128)S(1)}, f32[16,128,256]{1,2,0:T(8,128)}) %get-tuple-element.340, (s32[16]{0:T(128)S(1)}, s32[16,6]{0,1:T(8,128)S(1)}, bf16[48,2,128,256]{3,2,1,0:T(8,128)(2,1)}, ...), branch_computations={%region_13.15_spmd, %region_14.16_spmd} | conditional | flops 541066368 | bytes 52434416 | solution.py:89
  145.6 4.9 %gather_fusion.3 = bf16[16,2,128,256]{3,2,1,0:T(8,128)(2,1)} fusion(bf16[48,2,128,256]{3,2,1,0:T(8,128)(2,1)} %get-tuple-element.134, s32[1024]{0:T(1024)S(1)} %pad_clamp_fusion.3), kind=kCustom, calls=%fused_computation.3.clone | custom fusion | bytes 4194368 | tf_op jit(solution)/shard_map/cond/branch_1_fun/jit(_take)/gather | solution.py:79
  150.4 4.0 %copy.63 = bf16[16,2,128,256]{2,3,0,1:T(8,128)(2,1)} copy(bf16[16,2,128,256]{3,2,1,0:T(8,128)(2,1)} %gather_fusion.3) | data formatting | bytes 4194304 | tf_op jit(solution)/shard_map/cond/branch_1_fun/jit(_take)/gather | solution.py:79
  154.4 1.9 broadcast_select_fusion.3
  158.0 1.8 bitcast_add_fusion.6
  159.9 1.9 fusion.6
  161.8 1.9 bitcast_add_fusion.7
  163.6 18.3 %conditional.10 = ((f32[16,128,256]{1,2,0:T(8,128)S(1)}, f32[16,128,256]{1,2,0:T(8,128)})) conditional(s32[]{:T(128)} %convert_element_type.39, (f32[16,128,256]{1,2,0:T(8,128)S(1)}, f32[16,128,256]{1,2,0:T(8,128)}) %get-tuple-element.341, (s32[16]{0:T(128)S(1)}, s32[16,6]{0,1:T(8,128)S(1)}, bf16[48,2,128,256]{3,2,1,0:T(8,128)(2,1)}, ...), branch_computations={%region_15.17_spmd, %region_16.18_spmd} | conditional | flops 541066368 | bytes 52434416 | solution.py:89
  163.9 4.9 %gather_fusion.4 = bf16[16,2,128,256]{3,2,1,0:T(8,128)(2,1)} fusion(bf16[48,2,128,256]{3,2,1,0:T(8,128)(2,1)} %get-tuple-element.140, s32[1024]{0:T(1024)S(1)} %pad_clamp_fusion.4), kind=kCustom, calls=%fused_computation.4.clone | custom fusion | bytes 4194368 | tf_op jit(solution)/shard_map/cond/branch_1_fun/jit(_take)/gather | solution.py:79
  168.8 4.0 %copy.64 = bf16[16,2,128,256]{2,3,0,1:T(8,128)(2,1)} copy(bf16[16,2,128,256]{3,2,1,0:T(8,128)(2,1)} %gather_fusion.4) | data formatting | bytes 4194304 | tf_op jit(solution)/shard_map/cond/branch_1_fun/jit(_take)/gather | solution.py:79
  172.7 1.9 broadcast_select_fusion.4
  176.3 1.8 bitcast_add_fusion.8
  178.2 1.9 fusion.8
  180.1 1.9 bitcast_add_fusion.9
  182.0 22.3 %conditional.11 = (bf16[16,1,128,256]{3,2,1,0:T(8,128)(2,1)S(1)}, bf16[16,1,128,256]{3,2,1,0:T(8,128)(2,1)S(1)}) conditional(s32[]{:T(128)} %convert_element_type.38, (f32[16,128,256]{1,2,0:T(8,128)S(1)}, f32[16,128,256]{1,2,0:T(8,128)}) %get-tuple-element.342, (s32[16]{0:T(128)S(1)}, s32[16,6]{0,1:T(8,128)S(1)}, ...), branch_computations={%region_17.19_spmd, %region_18.20_spmd} | conditional | flops 542114944 | bytes 67114528 | solution.py:89
  182.0 4.9 %gather_fusion.5 = bf16[16,2,128,256]{3,2,1,0:T(8,128)(2,1)} fusion(bf16[48,2,128,256]{3,2,1,0:T(8,128)(2,1)} %get-tuple-element.146, s32[1024]{0:T(1024)S(1)} %pad_clamp_fusion.5), kind=kCustom, calls=%fused_computation.5.clone | custom fusion | bytes 4194368 | tf_op jit(solution)/shard_map/cond/branch_1_fun/jit(_take)/gather | solution.py:79
  186.9 4.0 %copy.65 = bf16[16,2,128,256]{2,3,0,1:T(8,128)(2,1)} copy(bf16[16,2,128,256]{3,2,1,0:T(8,128)(2,1)} %gather_fusion.5) | data formatting | bytes 4194304 | tf_op jit(solution)/shard_map/cond/branch_1_fun/jit(_take)/gather | solution.py:79
  190.9 1.9 broadcast_select_fusion.5
  192.7 2.0 fusion.15
  198.1 1.9 fusion.14
  200.2 2.5 %fusion.12 = bf16[16,1,128,256]{2,3,0,1:T(8,128)(2,1)} fusion(f32[16,128,256]{1,2,0:T(8,128)S(1)} %get-tuple-element.144, f32[16,256,128]{2,1,0:T(8,128)S(1)} %fusion.14, f32[16]{0:T(128)S(1)} %get-tuple-element.313, bf16[16,2,128,256]{2,3,0,1:T(8,128)(2,1)S(1)} %copy-done.12, bf16[16,6,2,128,128]{4,3,2,1,0:T(8,128)(2,1)} %get-tuple-element.283), kind=kOutput, calls=%fused_computation.79 | convolution fusion | flops 136314880 | bytes 6816256 | tf_op jit(solution)/shard_map/cond/branch_1_fun/lab,lbr->lar/dot_general | solution.py:18
  (115 shorter events, 36.3 us)
Async XLA Ops:
  6.5 8.9 %copy-start.13 = (bf16[16,2,128,256]{3,2,1,0:T(8,128)(2,1)S(1)}, bf16[16,2,128,256]{3,2,1,0:T(8,128)(2,1)}, u32[]{:S(2)}) copy-start(bf16[16,2,128,256]{3,2,1,0:T(8,128)(2,1)} %param.26) | copy-start | bytes 6291460
  6.5 8.9 %copy-start.20 = (bf16[16,2,32,128]{3,2,1,0:T(8,128)(2,1)S(1)}, bf16[16,2,32,128]{3,2,1,0:T(8,128)(2,1)}, u32[]{:S(2)}) copy-start(bf16[16,2,32,128]{3,2,1,0:T(8,128)(2,1)} %param.30) | copy-start | bytes 786436
  6.5 67.4 %all-reduce.2.cloned.1.call-start = ((), (), s32[]{:S(2)}) async-start(), calls=%async_computation | async-start | bytes 131072 | tf_op jit(solution)/shard_map/psum | solution.py:52
  6.5 76.7 %collective-permute-start = (bf16[16,2,128,256]{3,2,1,0:T(8,128)(2,1)}, bf16[16,2,128,256]{3,2,1,0:T(8,128)(2,1)}, u32[]{:S(2)}, u32[]{:S(2)}) collective-permute-start(bf16[16,2,128,256]{3,2,1,0:T(8,128)(2,1)} %param.26), channel_id=1, source_target_pairs={{0,1},{1,2},{2,3},{3,4},{4,5},{5,6},{6,7},{8,9},{9,10},{10,11},{11... | collective-permute-start | bytes 6291464 | tf_op jit(solution)/shard_map/ppermute | solution.py:12
  8.6 79.4 %collective-permute-start.1 = (bf16[16,2,128,256]{3,2,1,0:T(8,128)(2,1)}, bf16[16,2,128,256]{3,2,1,0:T(8,128)(2,1)}, u32[]{:S(2)}, u32[]{:S(2)}) collective-permute-start(bf16[16,2,128,256]{3,2,1,0:T(8,128)(2,1)} %param.26), channel_id=1, source_target_pairs={{1,0},{2,1},{3,2},{4,3},{5,4},{6,5},{7,6},{9,8},{10,9},{11,10},{12... | collective-permute-start | bytes 6291464 | tf_op jit(solution)/shard_map/ppermute | solution.py:12
  15.4 1.0 copy-start.17
  16.5 2.1 copy-start.22
  16.5 3.4 %copy-start.26 = (s32[1,7]{1,0:T(1,128)S(1)}, s32[1,7]{1,0:T(1,128)}, u32[]{:S(2)}) copy-start(s32[1,7]{1,0:T(1,128)} %param.32) | copy-start | bytes 88
  18.0 30.0 %copy-start.21 = (f32[1,7,2,32,32]{4,3,2,1,0:T(8,128)S(1)}, f32[1,7,2,32,32]{4,3,2,1,0:T(8,128)}, u32[]{:S(2)}) copy-start(f32[1,7,2,32,32]{4,3,2,1,0:T(8,128)} %param.35) | copy-start | bytes 172036
  19.9 29.5 %copy-start.25 = (s32[16,6]{0,1:T(8,128)S(1)}, s32[16,6]{0,1:T(8,128)}, u32[]{:S(2)}) copy-start(s32[16,6]{0,1:T(8,128)} %param.28) | copy-start | bytes 1156
  19.9 29.5 %copy-start.24 = (s32[16]{0:T(128)S(1)}, s32[16]{0:T(128)}, u32[]{:S(2)}) copy-start(s32[16]{0:T(128)} %param.29) | copy-start | bytes 196
  19.9 54.0 %copy-start.23 = (f32[1,2,32,32]{3,2,1,0:T(8,128)S(1)}, f32[1,2,32,32]{3,2,1,0:T(8,128)}, u32[]{:S(2)}) copy-start(f32[1,2,32,32]{3,2,1,0:T(8,128)} %param.34) | copy-start | bytes 24580
  19.9 55.9 %copy-start.18 = (f32[16,2,32,32]{3,2,1,0:T(8,128)S(1)}, f32[16,2,32,32]{3,2,1,0:T(8,128)}, u32[]{:S(2)}) copy-start(f32[16,2,32,32]{3,2,1,0:T(8,128)} %param.36) | copy-start | bytes 393220
  74.9 5.1 %copy-start.19 = (bf16[16,2,32,128]{3,2,1,0:T(8,128)(2,1)S(1)}, bf16[16,2,32,128]{3,2,1,0:T(8,128)(2,1)}, u32[]{:S(2)}) copy-start(bf16[16,2,32,128]{3,2,1,0:T(8,128)(2,1)} %param.37) | copy-start | bytes 786436
  83.2 3.3 %copy-start.14 = (bf16[16,2,128,256]{3,2,1,0:T(8,128)(2,1)S(1)}, bf16[16,2,128,256]{3,2,1,0:T(8,128)(2,1)}, u32[]{:S(2)}) copy-start(bf16[16,2,128,256]{3,2,1,0:T(8,128)(2,1)} %param.26) | copy-start | bytes 6291460
  101.9 1.8 copy-start
  105.5 3.8 %copy-start.1 = (f32[16,128,256]{1,2,0:T(8,128)}, f32[16,128,256]{1,2,0:T(8,128)S(1)}, u32[]{:S(2)}) copy-start(f32[16,128,256]{1,2,0:T(8,128)S(1)} %bitcast_add_fusion) | copy-start | bytes 6291460 | tf_op jit(solution)/shard_map/cond
  120.0 1.8 copy-start.2
  123.6 3.8 %copy-start.3 = (f32[16,128,256]{1,2,0:T(8,128)}, f32[16,128,256]{1,2,0:T(8,128)S(1)}, u32[]{:S(2)}) copy-start(f32[16,128,256]{1,2,0:T(8,128)S(1)} %bitcast_add_fusion.2) | copy-start | bytes 6291460 | tf_op jit(solution)/shard_map/cond
  138.1 1.8 copy-start.4
  141.7 3.8 %copy-start.5 = (f32[16,128,256]{1,2,0:T(8,128)}, f32[16,128,256]{1,2,0:T(8,128)S(1)}, u32[]{:S(2)}) copy-start(f32[16,128,256]{1,2,0:T(8,128)S(1)} %bitcast_add_fusion.4) | copy-start | bytes 6291460 | tf_op jit(solution)/shard_map/cond
  156.2 1.8 copy-start.6
  159.9 3.8 %copy-start.7 = (f32[16,128,256]{1,2,0:T(8,128)}, f32[16,128,256]{1,2,0:T(8,128)S(1)}, u32[]{:S(2)}) copy-start(f32[16,128,256]{1,2,0:T(8,128)S(1)} %bitcast_add_fusion.6) | copy-start | bytes 6291460 | tf_op jit(solution)/shard_map/cond
  174.6 1.8 copy-start.8
  178.2 3.8 %copy-start.9 = (f32[16,128,256]{1,2,0:T(8,128)}, f32[16,128,256]{1,2,0:T(8,128)S(1)}, u32[]{:S(2)}) copy-start(f32[16,128,256]{1,2,0:T(8,128)S(1)} %bitcast_add_fusion.8) | copy-start | bytes 6291460 | tf_op jit(solution)/shard_map/cond
  192.7 2.0 copy-start.11
  192.7 2.5 %copy-start.10 = (f32[16,128,256]{1,2,0:T(8,128)S(1)}, f32[16,128,256]{1,2,0:T(8,128)}, u32[]{:S(2)}) copy-start(f32[16,128,256]{1,2,0:T(8,128)} %get-tuple-element.149) | copy-start | bytes 6291460 | tf_op jit(solution)/shard_map/cond
  198.1 2.1 copy-start.12
  202.7 1.6 copy-start.16
Sparse Core Ops, SparseCore 0:
  20.0 53.8 all-reduce.1
where the time goes:
time: 217 us; the launch traced here: 213 us
  local copies, waits for them, and re-layouts  66 us (30%)
  matrix products  61 us (28%)
  blocking collectives  27.4 us (13%)
  waiting for transfers between devices  20 us (9%)
  between operations  17.6 us (8%)
  other arithmetic  14.2 us (7%)
  starting transfers between devices  5.69 us (3%)
    dot_general x52, matrix products, single(): jnp.einsum(pattern, left_side, right_side, precision=precision, preferred...  61 us
    gather x12, local copies, waits for them, and re-layouts, add_column(): pieces = jnp.take(extended, local_index[:, column], axis=0)  52.9 us
    all_gather x1, blocking collectives, shards(): root_coefs = lax.all_gather(root_stack, 'leaf', axis=0, tiled=True)  27.4 us
    psum x1, waiting for transfers between devices, shards(): global_sum = lax.psum(top_stack, 'leaf')  19.9 us
    select_n x6, other arithmetic, add_column(): pieces = jnp.take(extended, local_index[:, column], axis=0)  11.1 us
    ppermute x2, starting transfers between devices, from_behind(): return lax.ppermute(block, axis, route)  5.69 us
    unnamed x26, local copies, waits for them, and re-layouts  5.31 us
  transfers between devices with their start and end apart: 3, of which 1 were waited for; matrix products, arithmetic and copies ran while one was open for 11% of the time, Pallas kernels for 0%

commit v1 on v0

v1 whole, which is shorter than its diff:
```python
import functools

import jax
import jax.numpy as jnp
from jax import lax
from jax.experimental import pallas as pl
from jax.experimental.pallas import tpu as pltpu
from jax.sharding import PartitionSpec as P

HALO = 4
MESH = pl.DeviceIdType.MESH
F32 = jnp.float32
BF16 = jnp.bfloat16


def mul(left, right):
    return jnp.dot(left, right, preferred_element_type=F32)


def split(x):
    high = x.astype(BF16)
    return high, (x - high.astype(F32)).astype(BF16)


def pack(real, imag):
    rh, rl = split(real)
    ih, il = split(imag)
    return jnp.concatenate([rh, ih, rl, il], axis=1)


def operand(real, imag):
    minus = -imag
    left = jnp.concatenate([real, minus, real, minus], axis=0)
    right = jnp.concatenate([imag, real, imag, real], axis=0)
    return jnp.concatenate([left, right], axis=1)


def kernel(
    n,
    density,
    near_tiles,
    neighbours,
    counts,
    leaf_basis,
    leaf_transfer,
    admissible,
    top_out,
    top_in,
    coupling,
    down_transfer,
    out_basis,
    out,
    own,
    low,
    high,
    tiles,
    coef,
    msg,
    near,
    down,
    result,
    own_sem,
    tile_sem,
    side_sem,
    halo_send,
    halo_recv,
    root_send,
    root_recv,
    pass_send,
    pass_recv,
    out_sem,
):
    me = lax.axis_index("leaf")
    chips = n // 2
    chip = me // 2
    core = me % 2
    sibling = chip * 2 + (1 - core)
    leaves, _, panels, rhs = density.shape
    slots = near_tiles.shape[1]
    rank = leaf_basis.shape[2]
    far = coupling.shape[1]
    size = 2 * panels
    chunks = leaves // HALO
    inner = list(range(1, chunks - 1))
    order = inner + [0, chunks - 1]

    own_copies = [
        pltpu.make_async_copy(
            density.at[pl.ds(k * HALO, HALO)], own.at[pl.ds(k * HALO, HALO)], own_sem.at[k]
        )
        for k in range(chunks)
    ]
    tile_copies = [
        pltpu.make_async_copy(
            near_tiles.at[pl.ds(k * HALO, HALO)], tiles.at[pl.ds(k * HALO, HALO)], tile_sem.at[k]
        )
        for k in range(chunks)
    ]
    side_copies = [
        pltpu.make_async_copy(
            density.at[pl.ds(0, 2 * HALO)], low.at[pl.ds(HALO, 2 * HALO)], side_sem.at[0]
        ),
        pltpu.make_async_copy(
            density.at[pl.ds(leaves - 2 * HALO, 2 * HALO)],
            high.at[pl.ds(0, 2 * HALO)],
            side_sem.at[1],
        ),
    ]
    for copy in own_copies:
        copy.start()

    barrier = pltpu.get_barrier_semaphore()
    for step in range(1, n):
        pl.semaphore_signal(
            barrier, inc=1, device_id={"leaf": lax.rem(me + step, n)}, device_id_type=MESH
        )
    pl.semaphore_wait(barrier, n - 1)

    def halo_copy(source, target, which, to):
        return pltpu.make_async_remote_copy(
            src_ref=source,
            dst_ref=target,
            send_sem=halo_send.at[which],
            recv_sem=halo_recv.at[which],
            device_id={"leaf": to},
            device_id_type=MESH,
        )

    def to_below():
        return halo_copy(
            density.at[pl.ds(0, HALO)],
            high.at[pl.ds(2 * HALO, HALO)],
            1,
            lax.rem(me + n - 1, n),
        )

    def to_above():
        return halo_copy(
            density.at[pl.ds(leaves - HALO, HALO)], low.at[pl.ds(0, HALO)], 0, lax.rem(me + 1, n)
        )

    @pl.when(me > 0)
    def _():
        to_below().start()

    @pl.when(me < n - 1)
    def _():
        to_above().start()

    for k in order:
        tile_copies[k].start()
    for copy in side_copies:
        copy.start()

    def one_coef(leaf, carry):
        basis = leaf_basis[leaf]
        left = jnp.concatenate(
            [
                jnp.concatenate([basis[0], -basis[1]], axis=1),
                jnp.concatenate([basis[1], basis[0]], axis=1),
            ],
            axis=0,
        )
        value = mul(left, own[leaf].reshape(size, rhs))
        rows = pl.ds(pl.multiple_of(leaf * rank, rank), rank)
        coef[0, rows] = value[:rank]
        coef[1, rows] = value[rank:]
        return carry

    for k in range(chunks):
        own_copies[k].wait()
        lax.fori_loop(k * HALO, (k + 1) * HALO, one_coef, 0, unroll=True)

    upward = jnp.concatenate(
        [leaf_transfer[leaf].reshape(2 * rank, rank) for leaf in range(leaves)], axis=1
    )
    up_high, up_low = split(upward)
    up_both = jnp.concatenate([up_high, up_low], axis=0)

    def upward_sum(part):
        c_high, c_low = split(coef[part])
        first = mul(up_both, c_high)
        return first[: 2 * rank] + first[2 * rank :] + mul(up_high, c_low)

    sum_real, sum_imag = upward_sum(0), upward_sum(1)
    msg[me, :rank] = (sum_real[:rank] - sum_imag[rank:]).astype(BF16)
    msg[me, rank : 2 * rank] = (sum_real[rank:] + sum_imag[:rank]).astype(BF16)
    packed = pack(top_out[0, 0], top_out[0, 1])
    msg[me, 2 * rank :] = jnp.concatenate([packed[: rank // 2], packed[rank // 2 :]], axis=1)

    def root_copy(slot, send, recv, to):
        return pltpu.make_async_remote_copy(
            src_ref=msg.at[slot],
            dst_ref=msg.at[slot],
            send_sem=send,
            recv_sem=recv,
            device_id={"leaf": to},
            device_id_type=MESH,
        )

    direct = [root_copy(me, pass_send.at[0], pass_recv.at[0], sibling)]
    for step in range(1, chips):
        to = lax.rem(chip + step, chips) * 2 + core
        direct.append(root_copy(me, root_send.at[step], root_recv.at[step], to))
    for copy in direct:
        copy.start()

    def near_leaf(source, shift):
        first = me * leaves + shift
        count = source.shape[0]

        def body(leaf, carry):
            tops, bottoms, pieces = [], [], []
            for slot in range(slots):
                live = jnp.where(counts[leaf] > slot, 1.0, 0.0).astype(F32)
                live = jnp.full((panels, panels), live, F32).astype(BF16)
                real = tiles[leaf, slot, 0] * live
                imag = tiles[leaf, slot, 1] * live
                tops += [real, -imag]
                bottoms += [imag, real]
                place = jnp.clip(neighbours[slot, leaf] - first, 0, count - 1)
                pieces.append(source[place].reshape(size, rhs))
            left = jnp.concatenate(
                [jnp.concatenate(tops, axis=1), jnp.concatenate(bottoms, axis=1)], axis=0
            )
            near[leaf] = mul(left, jnp.concatenate(pieces, axis=0))
            return carry

        return body

    for k in inner:
        tile_copies[k].wait()
        lax.fori_loop(k * HALO, (k + 1) * HALO, near_leaf(own, 0), 0)

    passed = []
    for step in range(1, chips):
        slot = lax.rem(chip + chips - step, chips) * 2 + core
        direct[step].wait_recv()
        copy = root_copy(slot, pass_send.at[step], pass_recv.at[step], sibling)
        copy.start()
        passed.append(copy)

    tile_copies[0].wait()
    side_copies[0].wait()

    @pl.when(me > 0)
    def _():
        to_above().wait_recv()

    lax.fori_loop(0, HALO, near_leaf(low, -HALO), 0)
    tile_copies[chunks - 1].wait()
    side_copies[1].wait()

    @pl.when(me < n - 1)
    def _():
        to_below().wait_recv()

    lax.fori_loop(leaves - HALO, leaves, near_leaf(high, leaves - 2 * HALO), 0)

    d_high, d_low = split(down_transfer[...].reshape(leaves * 2 * rank, rank))
    downward = jnp.concatenate([d_high, d_low, d_high], axis=1)
    pairs = [pack(coupling[0, slot, 0], coupling[0, slot, 1]) for slot in range(far)]
    packed_in = pack(top_in[0, 0], top_in[0, 1])

    direct[0].wait_recv()
    for copy in passed:
        copy.wait_recv()

    tops, roots = [], []
    for d in range(n):
        piece = msg[d, 2 * rank :]
        tops.append(jnp.concatenate([piece[:, : size // 2], piece[:, size // 2 :]], axis=0))
        roots.append(operand(msg[d, :rank], msg[d, rank : 2 * rank]))
    top = mul(jnp.concatenate(tops, axis=1), jnp.concatenate(roots, axis=0))
    top_high, top_low = split(top)
    picked = []
    for slot in range(far):
        value = msg[admissible[0, slot]]
        picked.append(operand(value[:rank], value[rank : 2 * rank]))
    field = mul(jnp.concatenate(pairs, axis=1), jnp.concatenate(picked, axis=0))
    field += mul(packed_in, operand(top_high[:, :rhs], top_high[:, rhs:]))
    field += mul(packed_in, operand(top_low[:, :rhs], top_low[:, rhs:]))
    f_high, f_low = split(field)
    down[...] = mul(downward, jnp.concatenate([f_high, f_high, f_low], axis=0))

    def finish(leaf, carry):
        rows = pl.multiple_of(leaf * 2 * rank, 2 * rank)
        upper = down[pl.ds(rows, rank)]
        lower = down[pl.ds(rows + rank, rank)]
        coefs = jnp.concatenate(
            [upper[:, :rhs] - lower[:, rhs:], lower[:, :rhs] + upper[:, rhs:]], axis=0
        ).astype(BF16)
        basis = out_basis[leaf]
        left = jnp.concatenate(
            [
                jnp.concatenate([basis[0], basis[1]], axis=1),
                jnp.concatenate([-basis[1], basis[0]], axis=1),
            ],
            axis=0,
        )
        value = lax.dot_general(left, coefs, (((0,), (0,)), ((), ())), preferred_element_type=F32)
        result[leaf] = (value + near[leaf]).astype(BF16).reshape(2, panels, rhs)
        return carry

    outs = []
    for k in range(chunks):
        lax.fori_loop(k * HALO, (k + 1) * HALO, finish, 0, unroll=True)
        copy = pltpu.make_async_copy(
            result.at[pl.ds(k * HALO, HALO)], out.at[pl.ds(k * HALO, HALO)], out_sem.at[k]
        )
        copy.start()
        outs.append(copy)

    @pl.when(me > 0)
    def _():
        to_below().wait_send()

    @pl.when(me < n - 1)
    def _():
        to_above().wait_send()

    for copy in direct + passed:
        copy.wait_send()
    for copy in outs:
        copy.wait()


def shards(*args):
    density, near_tiles = args[0], args[1]
    leaf_basis = args[4]
    n = lax.axis_size("leaf")
    leaves, _, panels, rhs = density.shape
    rank = leaf_basis.shape[2]
    chunks = leaves // HALO
    hbm = pl.BlockSpec(memory_space=pl.ANY)
    vmem = pl.BlockSpec(memory_space=pltpu.VMEM)
    smem = pl.BlockSpec(memory_space=pltpu.SMEM)
    dma = pltpu.SemaphoreType.DMA
    return pl.pallas_call(
        functools.partial(kernel, n),
        out_shape=jax.ShapeDtypeStruct(density.shape, BF16),
        in_specs=[hbm, hbm, smem, smem, vmem, vmem, smem, vmem, vmem, vmem, vmem, vmem],
        out_specs=hbm,
        scratch_shapes=[
            pltpu.VMEM(density.shape, BF16),
            pltpu.VMEM((3 * HALO,) + density.shape[1:], BF16),
            pltpu.VMEM((3 * HALO,) + density.shape[1:], BF16),
            pltpu.VMEM(near_tiles.shape, BF16),
            pltpu.VMEM((2, leaves * rank, rhs), F32),
            pltpu.VMEM((n, 2 * rank + rank // 2, rhs), BF16),
            pltpu.VMEM((leaves, 2 * panels, rhs), F32),
            pltpu.VMEM((leaves * 2 * rank, 2 * rhs), F32),
            pltpu.VMEM(density.shape, BF16),
            dma((chunks,)),
            dma((chunks,)),
            dma((2,)),
            dma((2,)),
            dma((2,)),
            dma((n // 2,)),
            dma((n // 2,)),
            dma((n // 2,)),
            dma((n // 2,)),
            dma((chunks,)),
        ],
        compiler_params=pltpu.CompilerParams(
            collective_id=0, has_side_effects=True, vmem_limit_bytes=62 * 1024 * 1024
        ),
    )(*args[:2], args[2].T, *args[3:])


def solution(mesh):
    in_specs = (
        P("leaf", "node", None, None),
        P("leaf", None, "node", None, None),
        P("leaf", None),
        P("leaf"),
        P("leaf", "node", None, None),
        P("leaf", "node", None, None),
        P("leaf", None),
        P("leaf", "node", None, None),
        P("leaf", "node", None, None),
        P("leaf", None, "node", None, None),
        P("leaf", "node", None, None),
        P("leaf", "node", None, None),
    )
    out_specs = P("leaf", "node", None, None)
    return jax.shard_map(shards, mesh=mesh, in_specs=in_specs, out_specs=out_specs, check_vma=False)
```

time: 217 us -> 27.4 us (0.13)
  the two profiles are of different devices: /device:TPU:24 before, /device:TPU:0 now
where the time goes in v1:
time: 27.4 us; the launch traced here: 27.3 us
  Pallas kernels  24.1 us (88%)
  local copies, waits for them, and re-layouts  3.13 us (11%)
    pallas_call x1, Pallas kernels, shards(): pl.pallas_call(functools.partial(kernel, n), out_shape=jax.ShapeDtypeStru...  24.1 us
    unnamed x1, local copies, waits for them, and re-layouts  3.13 us

profile of v1, /device:TPU:0, one launch (start us, length us, event | category | flops | bytes accessed | tf_op | source)
XLA Modules:
  0.0 27.3 jit_solution(10636747217307004409)
XLA Ops:
  0.0 24.1 %shard_map.118 = bf16[16,2,128,256]{3,2,1,0:T(8,128)(2,1)} custom-call(bf16[16,2,128,256]{3,2,1,0:T(8,128)(2,1)} %density.1, bf16[16,6,2,128,128]{4,3,2,1,0:T(8,128)(2,1)} %near_tiles.1, s32[6,16]{1,0:T(8,128)} %bitcast.1, s32[16]{0:T(128)} %counts.1, bf16[16,2,32,128]{3,2,1,0:T(8,128)(2,1)} %leaf_basis.1, f32[16,2,32,32]{3,2,1,0:T(8,128)} %leaf_transfer.1, ...), custom_call_target="tpu_custom_call" | custom-call | tf_op jit(solution)/shard_map/pallas_call | solution.py:339
  24.1 3.1 %copy.14 = bf16[16,2,128,256]{3,2,1,0:T(8,128)(2,1)} copy(bf16[16,2,128,256]{3,2,1,0:T(8,128)(2,1)} %shard_map.118) | data formatting | bytes 4194304

commit v2 on v1

--- a/solution.py
+++ b/solution.py
@@ -8,6 +8,8 @@
 from jax.sharding import PartitionSpec as P
 
 HALO = 4
+LIVE = 3
+INDICES = (2, 3, 6)
 MESH = pl.DeviceIdType.MESH
 F32 = jnp.float32
 BF16 = jnp.bfloat16
@@ -39,6 +41,17 @@
     n,
     density,
     near_tiles,
+    neighbours_far,
+    counts_far,
+    leaf_basis_far,
+    leaf_transfer_far,
+    admissible_far,
+    top_out_far,
+    top_in_far,
+    coupling_far,
+    down_transfer_far,
+    out_basis_far,
+    out,
     neighbours,
     counts,
     leaf_basis,
@@ -49,7 +62,8 @@
     coupling,
     down_transfer,
     out_basis,
-    out,
+    turned,
+    small_sem,
     own,
     low,
     high,
@@ -58,7 +72,6 @@
     msg,
     near,
     down,
-    result,
     own_sem,
     tile_sem,
     side_sem,
@@ -68,7 +81,6 @@
     root_recv,
     pass_send,
     pass_recv,
-    out_sem,
 ):
     me = lax.axis_index("leaf")
     chips = n // 2
@@ -106,14 +118,60 @@
             side_sem.at[1],
         ),
     ]
-    for copy in own_copies:
-        copy.start()
-
+    small = [
+        (leaf_basis_far, leaf_basis),
+        (leaf_transfer_far, leaf_transfer),
+        (top_out_far, top_out),
+        (top_in_far, top_in),
+        (coupling_far, coupling),
+        (down_transfer_far, down_transfer),
+        (out_basis_far, out_basis),
+        (neighbours_far, neighbours),
+        (counts_far, counts),
+        (admissible_far, admissible),
+    ]
+    small_copies = [
+        pltpu.make_async_copy(source, target, small_sem.at[k])
+        for k, (source, target) in enumerate(small)
+    ]
     barrier = pltpu.get_barrier_semaphore()
     for step in range(1, n):
         pl.semaphore_signal(
             barrier, inc=1, device_id={"leaf": lax.rem(me + step, n)}, device_id_type=MESH
         )
+    small_copies[0].start()
+    for copy in own_copies:
+        copy.start()
+    for copy in small_copies[1:]:
+        copy.start()
+    for k in order:
+        tile_copies[k].start()
+    for copy in side_copies:
+        copy.start()
+
+    def one_coef(leaf, carry):
+        basis = leaf_basis[leaf]
+        left = jnp.concatenate(
+            [
+                jnp.concatenate([basis[0], -basis[1]], axis=1),
+                jnp.concatenate([basis[1], basis[0]], axis=1),
+            ],
+            axis=0,
+        )
+        value = mul(left, own[leaf].reshape(size, rhs))
+        rows = pl.ds(pl.multiple_of(leaf * rank, rank), rank)
+        coef[0, rows] = value[:rank]
+        coef[1, rows] = value[rank:]
+        return carry
+
+    def coefs_of(k):
+        own_copies[k].wait()
+        lax.fori_loop(k * HALO, (k + 1) * HALO, one_coef, 0, unroll=True)
+
+    early = chunks // 2
+    small_copies[0].wait()
+    for k in range(early):
+        coefs_of(k)
     pl.semaphore_wait(barrier, n - 1)
 
     def halo_copy(source, target, which, to):
@@ -147,30 +205,10 @@
     def _():
         to_above().start()
 
-    for k in order:
-        tile_copies[k].start()
-    for copy in side_copies:
-        copy.start()
-
-    def one_coef(leaf, carry):
-        basis = leaf_basis[leaf]
-        left = jnp.concatenate(
-            [
-                jnp.concatenate([basis[0], -basis[1]], axis=1),
-                jnp.concatenate([basis[1], basis[0]], axis=1),
-            ],
-            axis=0,
-        )
-        value = mul(left, own[leaf].reshape(size, rhs))
-        rows = pl.ds(pl.multiple_of(leaf * rank, rank), rank)
-        coef[0, rows] = value[:rank]
-        coef[1, rows] = value[rank:]
-        return carry
-
-    for k in range(chunks):
-        own_copies[k].wait()
-        lax.fori_loop(k * HALO, (k + 1) * HALO, one_coef, 0, unroll=True)
-
+    for k in range(early, chunks):
+        coefs_of(k)
+    small_copies[1].wait()
+    small_copies[2].wait()
     upward = jnp.concatenate(
         [leaf_transfer[leaf].reshape(2 * rank, rank) for leaf in range(leaves)], axis=1
     )
@@ -212,10 +250,13 @@
         def body(leaf, carry):
             tops, bottoms, pieces = [], [], []
             for slot in range(slots):
-                live = jnp.where(counts[leaf] > slot, 1.0, 0.0).astype(F32)
-                live = jnp.full((panels, panels), live, F32).astype(BF16)
-                real = tiles[leaf, slot, 0] * live
-                imag = tiles[leaf, slot, 1] * live
+                real = tiles[leaf, slot, 0]
+                imag = tiles[leaf, slot, 1]
+                if slot >= LIVE:
+                    live = jnp.where(counts[leaf] > slot, 1.0, 0.0).astype(F32)
+                    live = jnp.full((panels, panels), live, F32).astype(BF16)
+                    real *= live
+                    imag *= live
                 tops += [real, -imag]
                 bottoms += [imag, real]
                 place = jnp.clip(neighbours[slot, leaf] - first, 0, count - 1)
@@ -228,9 +269,22 @@
 
         return body
 
+    small_copies[7].wait()
+    small_copies[8].wait()
     for k in inner:
         tile_copies[k].wait()
-        lax.fori_loop(k * HALO, (k + 1) * HALO, near_leaf(own, 0), 0)
+        lax.fori_loop(k * HALO, (k + 1) * HALO, near_leaf(own, 0), 0, unroll=2)
+
+    small_copies[6].wait()
+
+    def turn(leaf, carry):
+        basis = out_basis[leaf].astype(F32)
+        left = jnp.concatenate([basis[0], -basis[1]], axis=0)
+        right = jnp.concatenate([basis[1], basis[0]], axis=0)
+        turned[leaf] = jnp.concatenate([left, right], axis=1).T.astype(BF16)
+        return carry
+
+    lax.fori_loop(0, leaves, turn, 0, unroll=2)
 
     passed = []
     for step in range(1, chips):
@@ -247,7 +301,7 @@
     def _():
         to_above().wait_recv()
 
-    lax.fori_loop(0, HALO, near_leaf(low, -HALO), 0)
+    lax.fori_loop(0, HALO, near_leaf(low, -HALO), 0, unroll=2)
     tile_copies[chunks - 1].wait()
     side_copies[1].wait()
 
@@ -255,8 +309,10 @@
     def _():
         to_below().wait_recv()
 
-    lax.fori_loop(leaves - HALO, leaves, near_leaf(high, leaves - 2 * HALO), 0)
-
+    lax.fori_loop(leaves - HALO, leaves, near_leaf(high, leaves - 2 * HALO), 0, unroll=2)
+
+    for copy in small_copies[3:6] + small_copies[9:]:
+        copy.wait()
     d_high, d_low = split(down_transfer[...].reshape(leaves * 2 * rank, rank))
     downward = jnp.concatenate([d_high, d_low, d_high], axis=1)
     pairs = [pack(coupling[0, slot, 0], coupling[0, slot, 1]) for slot in range(far)]
@@ -290,26 +346,11 @@
         coefs = jnp.concatenate(
             [upper[:, :rhs] - lower[:, rhs:], lower[:, :rhs] + upper[:, rhs:]], axis=0
         ).astype(BF16)
-        basis = out_basis[leaf]
-        left = jnp.concatenate(
-            [
-                jnp.concatenate([basis[0], basis[1]], axis=1),
-                jnp.concatenate([-basis[1], basis[0]], axis=1),
-            ],
-            axis=0,
-        )
-        value = lax.dot_general(left, coefs, (((0,), (0,)), ((), ())), preferred_element_type=F32)
-        result[leaf] = (value + near[leaf]).astype(BF16).reshape(2, panels, rhs)
+        value = mul(turned[leaf], coefs)
+        out[leaf] = (value + near[leaf]).astype(BF16).reshape(2, panels, rhs)
         return carry
 
-    outs = []
-    for k in range(chunks):
-        lax.fori_loop(k * HALO, (k + 1) * HALO, finish, 0, unroll=True)
-        copy = pltpu.make_async_copy(
-            result.at[pl.ds(k * HALO, HALO)], out.at[pl.ds(k * HALO, HALO)], out_sem.at[k]
-        )
-        copy.start()
-        outs.append(copy)
+    lax.fori_loop(0, leaves, finish, 0, unroll=4)
 
     @pl.when(me > 0)
     def _():
@@ -321,8 +362,6 @@
 
     for copy in direct + passed:
         copy.wait_send()
-    for copy in outs:
-        copy.wait()
 
 
 def shards(*args):
@@ -332,16 +371,24 @@
     leaves, _, panels, rhs = density.shape
     rank = leaf_basis.shape[2]
     chunks = leaves // HALO
-    hbm = pl.BlockSpec(memory_space=pl.ANY)
+    hbm = pl.BlockSpec(memory_space=pltpu.HBM)
     vmem = pl.BlockSpec(memory_space=pltpu.VMEM)
-    smem = pl.BlockSpec(memory_space=pltpu.SMEM)
     dma = pltpu.SemaphoreType.DMA
+    operands = [args[2].T if k == 2 else arg for k, arg in enumerate(args)]
+    for k in range(len(operands)):
+        operands[k] = pltpu.with_memory_space_constraint(operands[k], pltpu.HBM)
     return pl.pallas_call(
         functools.partial(kernel, n),
         out_shape=jax.ShapeDtypeStruct(density.shape, BF16),
-        in_specs=[hbm, hbm, smem, smem, vmem, vmem, smem, vmem, vmem, vmem, vmem, vmem],
-        out_specs=hbm,
+        in_specs=[hbm] * len(operands),
+        out_specs=vmem,
         scratch_shapes=[
+            (pltpu.SMEM if k in INDICES else pltpu.VMEM)(operands[k].shape, operands[k].dtype)
+            for k in range(2, len(operands))
+        ]
+        + [
+            pltpu.VMEM((leaves, 2 * panels, 2 * rank), BF16),
+            dma((len(operands) - 2,)),
             pltpu.VMEM(density.shape, BF16),
             pltpu.VMEM((3 * HALO,) + density.shape[1:], BF16),
             pltpu.VMEM((3 * HALO,) + density.shape[1:], BF16),
@@ -350,7 +397,6 @@
             pltpu.VMEM((n, 2 * rank + rank // 2, rhs), BF16),
             pltpu.VMEM((leaves, 2 * panels, rhs), F32),
             pltpu.VMEM((leaves * 2 * rank, 2 * rhs), F32),
-            pltpu.VMEM(density.shape, BF16),
             dma((chunks,)),
             dma((chunks,)),
             dma((2,)),
@@ -360,12 +406,11 @@
             dma((n // 2,)),
             dma((n // 2,)),
             dma((n // 2,)),
-            dma((chunks,)),
         ],
         compiler_params=pltpu.CompilerParams(
-            collective_id=0, has_side_effects=True, vmem_limit_bytes=62 * 1024 * 1024
+            collective_id=0, has_side_effects=True, vmem_limit_bytes=40 * 1024 * 1024
         ),
-    )(*args[:2], args[2].T, *args[3:])
+    )(*operands)
 
 
 def solution(mesh):

time: 27.4 us -> 23.5 us (0.86)
  Pallas kernels: 24.1 us -> 22.1 us
  local copies, waits for them, and re-layouts: 3.13 us -> 1.32 us
    pallas_call x1, Pallas kernels: 24.1 us -> 22.1 us  [shards(): pl.pallas_call(functools.partial(kernel, n), out_shape=jax.ShapeDtypeStru...]
    unnamed x1, local copies, waits for them, and re-layouts: 3.13 us -> 1.32 us
where the time goes in v2:
time: 23.5 us; the launch traced here: 23.4 us
  Pallas kernels  22.1 us (94%)
  local copies, waits for them, and re-layouts  1.32 us (6%)
    pallas_call x1, Pallas kernels, shards(): pl.pallas_call(functools.partial(kernel, n), out_shape=jax.ShapeDtypeStru...  22.1 us
    unnamed x1, local copies, waits for them, and re-layouts  1.32 us

profile of v2, /device:TPU:0, one launch (start us, length us, event | category | flops | bytes accessed | tf_op | source)
XLA Modules:
  0.0 23.4 jit_solution(9640903244826278220)
XLA Ops:
  0.0 22.1 %shard_map.118 = bf16[16,2,128,256]{3,2,1,0:T(8,128)(2,1)S(1)} custom-call(bf16[16,2,128,256]{3,2,1,0:T(8,128)(2,1)} %density.1, bf16[16,6,2,128,128]{4,3,2,1,0:T(8,128)(2,1)} %near_tiles.1, s32[6,16]{1,0:T(8,128)} %bitcast.1, s32[16]{0:T(128)} %counts_far.1, bf16[16,2,32,128]{3,2,1,0:T(8,128)(2,1)} %leaf_basis_far.1, f32[16,2,32,32]{3,2,1,0:T(8,128)} %leaf_transfer_far.1, ...), custom_call_target="tpu_custom_call" | custom-call | tf_op jit(solution)/shard_map/pallas_call | solution.py:380
  22.1 1.3 %copy.14 = bf16[16,2,128,256]{3,2,1,0:T(8,128)(2,1)} copy(bf16[16,2,128,256]{3,2,1,0:T(8,128)(2,1)S(1)} %shard_map.118) | data formatting | bytes 4194304

commit v3 on v2

--- a/solution.py
+++ b/solution.py
@@ -63,6 +63,9 @@
     down_transfer,
     out_basis,
     turned,
+    downward,
+    paired,
+    packed_in,
     small_sem,
     own,
     low,
@@ -168,10 +171,6 @@
         own_copies[k].wait()
         lax.fori_loop(k * HALO, (k + 1) * HALO, one_coef, 0, unroll=True)
 
-    early = chunks // 2
-    small_copies[0].wait()
-    for k in range(early):
-        coefs_of(k)
     pl.semaphore_wait(barrier, n - 1)
 
     def halo_copy(source, target, which, to):
@@ -205,7 +204,8 @@
     def _():
         to_above().start()
 
-    for k in range(early, chunks):
+    small_copies[0].wait()
+    for k in range(chunks):
         coefs_of(k)
     small_copies[1].wait()
     small_copies[2].wait()
@@ -286,6 +286,22 @@
 
     lax.fori_loop(0, leaves, turn, 0, unroll=2)
 
+    for copy in small_copies[3:6] + small_copies[9:]:
+        copy.wait()
+    d_high, d_low = split(down_transfer[...].reshape(leaves * 2 * rank, rank))
+    downward[...] = jnp.concatenate([d_high, d_low, d_high], axis=1)
+    pairs = [pack(coupling[0, slot, 0], coupling[0, slot, 1]) for slot in range(far)]
+    packed_in[...] = pack(top_in[0, 0], top_in[0, 1])
+    paired[...] = jnp.concatenate(pairs, axis=1)
+
+    tile_copies[0].wait()
+    side_copies[0].wait()
+
+    @pl.when(me > 0)
+    def _():
+        to_above().wait_recv()
+
+    lax.fori_loop(0, HALO, near_leaf(low, -HALO), 0, unroll=2)
     passed = []
     for step in range(1, chips):
         slot = lax.rem(chip + chips - step, chips) * 2 + core
@@ -294,14 +310,6 @@
         copy.start()
         passed.append(copy)
 
-    tile_copies[0].wait()
-    side_copies[0].wait()
-
-    @pl.when(me > 0)
-    def _():
-        to_above().wait_recv()
-
-    lax.fori_loop(0, HALO, near_leaf(low, -HALO), 0, unroll=2)
     tile_copies[chunks - 1].wait()
     side_copies[1].wait()
 
@@ -310,13 +318,6 @@
         to_below().wait_recv()
 
     lax.fori_loop(leaves - HALO, leaves, near_leaf(high, leaves - 2 * HALO), 0, unroll=2)
-
-    for copy in small_copies[3:6] + small_copies[9:]:
-        copy.wait()
-    d_high, d_low = split(down_transfer[...].reshape(leaves * 2 * rank, rank))
-    downward = jnp.concatenate([d_high, d_low, d_high], axis=1)
-    pairs = [pack(coupling[0, slot, 0], coupling[0, slot, 1]) for slot in range(far)]
-    packed_in = pack(top_in[0, 0], top_in[0, 1])
 
     direct[0].wait_recv()
     for copy in passed:
@@ -333,11 +334,11 @@
     for slot in range(far):
         value = msg[admissible[0, slot]]
         picked.append(operand(value[:rank], value[rank : 2 * rank]))
-    field = mul(jnp.concatenate(pairs, axis=1), jnp.concatenate(picked, axis=0))
-    field += mul(packed_in, operand(top_high[:, :rhs], top_high[:, rhs:]))
-    field += mul(packed_in, operand(top_low[:, :rhs], top_low[:, rhs:]))
+    field = mul(paired[...], jnp.concatenate(picked, axis=0))
+    field += mul(packed_in[...], operand(top_high[:, :rhs], top_high[:, rhs:]))
+    field += mul(packed_in[...], operand(top_low[:, :rhs], top_low[:, rhs:]))
     f_high, f_low = split(field)
-    down[...] = mul(downward, jnp.concatenate([f_high, f_high, f_low], axis=0))
+    down[...] = mul(downward[...], jnp.concatenate([f_high, f_high, f_low], axis=0))
 
     def finish(leaf, carry):
         rows = pl.multiple_of(leaf * 2 * rank, 2 * rank)
@@ -388,6 +389,9 @@
         ]
         + [
             pltpu.VMEM((leaves, 2 * panels, 2 * rank), BF16),
+            pltpu.VMEM((leaves * 2 * rank, 3 * rank), BF16),
+            pltpu.VMEM((rank, args[9].shape[1] * 4 * rank), BF16),
+            pltpu.VMEM((rank, 4 * rank), BF16),
             dma((len(operands) - 2,)),
             pltpu.VMEM(density.shape, BF16),
             pltpu.VMEM((3 * HALO,) + density.shape[1:], BF16),

time: 23.5 us -> 21.2 us (0.902)
  Pallas kernels: 22.1 us -> 19.8 us
    pallas_call x1, Pallas kernels: 22.1 us -> 19.8 us  [shards(): pl.pallas_call(functools.partial(kernel, n), out_shape=jax.ShapeDtypeStru...]
where the time goes in v3:
time: 21.2 us; the launch traced here: 21.1 us
  Pallas kernels  19.8 us (93%)
  local copies, waits for them, and re-layouts  1.32 us (6%)
    pallas_call x1, Pallas kernels, shards(): pl.pallas_call(functools.partial(kernel, n), out_shape=jax.ShapeDtypeStru...  19.8 us
    unnamed x1, local copies, waits for them, and re-layouts  1.32 us

profile of v3, /device:TPU:0, one launch (start us, length us, event | category | flops | bytes accessed | tf_op | source)
XLA Modules:
  0.0 21.1 jit_solution(13963620155748071797)
XLA Ops:
  0.0 19.8 %shard_map.118 = bf16[16,2,128,256]{3,2,1,0:T(8,128)(2,1)S(1)} custom-call(bf16[16,2,128,256]{3,2,1,0:T(8,128)(2,1)} %density.1, bf16[16,6,2,128,128]{4,3,2,1,0:T(8,128)(2,1)} %near_tiles.1, s32[6,16]{1,0:T(8,128)} %bitcast.1, s32[16]{0:T(128)} %counts_far.1, bf16[16,2,32,128]{3,2,1,0:T(8,128)(2,1)} %leaf_basis_far.1, f32[16,2,32,32]{3,2,1,0:T(8,128)} %leaf_transfer_far.1, ...), custom_call_target="tpu_custom_call" | custom-call | tf_op jit(solution)/shard_map/pallas_call | solution.py:381
  19.8 1.3 %copy.14 = bf16[16,2,128,256]{3,2,1,0:T(8,128)(2,1)} copy(bf16[16,2,128,256]{3,2,1,0:T(8,128)(2,1)S(1)} %shard_map.118) | data formatting | bytes 4194304
